TPU v7x, 256 devices: a whole 4x4x8 slice. The times are simulated.
256 devices in a mesh: row: 16 (over z, core), col: 16 (over x, y).
Axes of the slice: x: 4, y: 4, z: 8, core: 2. Of those that a mesh axis runs over, the one named last changes fastest.
Arguments:
- child_samples: bfloat16 [2, 2, 256, 262144], P(None, None, 'col', 'row'), may hold values from -6 to 6
- child_map: int32 [2, 2048], P(None, 'row'), may hold values from 0 to 127, as said below
- forward_probe: bfloat16 [256, 262144], P(None, ('row', 'col')), may hold values from -6 to 6
- adjoint_probe: bfloat16 [256, 262144], P(None, ('row', 'col')), may hold values from -6 to 6
- stored_sparse_blocks: bfloat16 [2048, 18, 128, 128], P(('row', 'col')), may hold values from -0.125 to 0.125
- block_pattern: int32 [16, 128, 18], P(None, 'col'), may hold values from 0 to 7
Outputs:
- row_basis: bfloat16 [256, 262144], P(None, ('row', 'col'))
- column_basis: bfloat16 [256, 262144], P(None, ('row', 'col'))
- transfers: float32 [2, 2, 65536, 256], P(None, None, ('row', 'col'))
Inputs may be any that keep to these rules, and one draw needn't show every extreme that they name: Within each aligned group of 16 * 8 front blocks (one row group), each row of child_map is a permutation of 0 to 16 * 8 - 1.
All inputs are finite; a program needn't handle non-finite values.
Results may differ from a plain program's by a relative error of at most 0.0055.
Values may be sent and summed in bfloat16 or wider, within the bound.
A program may use at most 128 MiB of HBM per device.

v0:
```python
from functools import partial
import math
import jax
import jax.numpy as jnp
from jax import lax
from jax.sharding import PartitionSpec as P

S = 256
BLK = 128
SLOTS = 6


def padded(x, sides, width):
    for axis, dim in sides:
        peers, length = (lax.axis_size(axis), x.shape[dim])
        up = [(i, (i + 1) % peers) for i in range(peers - 1)]
        down = [(j, i) for i, j in up]
        last = lax.slice_in_dim(x, length - width, length, axis=dim)
        leading = lax.slice_in_dim(x, 0, width, axis=dim)
        before = lax.ppermute(last, axis, up)
        after = lax.ppermute(leading, axis, down)
        x = jnp.concatenate([before, x, after], axis=dim)
    return x


def shifted(block, axis, distance):
    devices = range(lax.axis_size(axis))
    route = [(i - distance, i) for i in devices if i - distance in devices]
    return lax.ppermute(block, axis, route)


def from_partner(value, axis, bit):
    mask = 2**bit
    pairs = [(source, source ^ mask) for source in range(lax.axis_size(axis))]
    return lax.ppermute(value, axis, pairs)


def spread_terms(targets, sketch_products, width):
    onehot = (targets[..., None] == jnp.arange(width, dtype=jnp.int32)).astype(jnp.float32)
    return jnp.einsum("bkg,bksc->sgc", onehot, sketch_products, precision=lax.Precision.HIGHEST)


def local(
    child_samples, child_map, forward_probe, adjoint_probe, stored_sparse_blocks, block_pattern
):
    samples_here = child_samples.shape[2]
    rows_group = child_samples.shape[3]
    group_blocks = rows_group // BLK
    leaf_rows = forward_probe.shape[1]
    leaf_blocks = leaf_rows // BLK
    row_pos = lax.axis_index("row")
    blocked = child_samples.reshape(2, 2, samples_here, group_blocks, BLK)
    first_child = jnp.take(blocked[0], child_map[0], axis=2).astype(jnp.float32)
    second_child = jnp.take(blocked[1], child_map[1], axis=2).astype(jnp.float32)
    extended = (
        (first_child + second_child).astype(jnp.bfloat16).reshape(2, samples_here, rows_group)
    )
    regrouped = lax.all_to_all(extended, "col", split_axis=2, concat_axis=1, tiled=True)
    own_pattern = lax.dynamic_index_in_dim(block_pattern, row_pos, 0, keepdims=False)
    regions = jnp.arange(3 * SLOTS, dtype=jnp.int32) // SLOTS
    flat_index = regions[None, :] * leaf_blocks + own_pattern
    probe_ext = padded(forward_probe, (("row", 1),), leaf_rows)
    conjugate_transpose_rows = adjoint_probe.reshape(S, leaf_blocks, BLK)
    sketch_products = jnp.einsum(
        "mda,duai->dumi",
        conjugate_transpose_rows,
        stored_sparse_blocks,
        preferred_element_type=jnp.float32,
    )
    terms = spread_terms(flat_index, sketch_products, 3 * leaf_blocks).reshape(S, 3, leaf_rows)
    from_above = shifted(terms[:, 0].astype(jnp.bfloat16), "row", -1).astype(jnp.float32)
    from_below = shifted(terms[:, 2].astype(jnp.bfloat16), "row", 1).astype(jnp.float32)
    adjoint_sparse = terms[:, 1] + from_above + from_below
    probe_blocks = probe_ext.reshape(S, 3 * leaf_blocks, BLK)
    selector = (flat_index[..., None] == jnp.arange(3 * leaf_blocks, dtype=jnp.int32)).astype(
        jnp.bfloat16
    )
    collected_samples = jnp.einsum(
        "jhc,wct->wjht", selector, probe_blocks, preferred_element_type=jnp.float32
    ).astype(jnp.bfloat16)
    forward_sparse = jnp.einsum(
        "wjht,jhot->wjo",
        collected_samples,
        stored_sparse_blocks,
        preferred_element_type=jnp.float32,
    ).reshape(S, leaf_rows)
    samples = jnp.stack(
        [
            regrouped[0].astype(jnp.float32) + forward_sparse,
            regrouped[1].astype(jnp.float32) + adjoint_sparse,
        ]
    )
    grams = jnp.einsum("ksr,ktr->kst", samples, samples, precision=lax.Precision.HIGHEST)
    level_one = grams + from_partner(grams.astype(jnp.bfloat16), "col", 0).astype(grams.dtype)
    level_two = level_one + from_partner(level_one.astype(jnp.bfloat16), "col", 1).astype(
        level_one.dtype
    )
    stacked_grams = jnp.concatenate([grams, level_one, level_two], axis=0)
    factors = jnp.linalg.cholesky(stacked_grams)
    identity = jnp.broadcast_to(jnp.eye(S, dtype=jnp.float32), factors.shape)
    inverses = jax.vmap(partial(jax.scipy.linalg.solve_triangular, lower=True))(factors, identity)
    factor_leaf = factors[0:2]
    factor_one = factors[2:4]
    inverse_leaf = inverses[0:2]
    inverse_one = inverses[2:4]
    inverse_two = inverses[4:6]
    bases = (
        jnp.einsum("kst,ktr->ksr", inverse_leaf, samples, precision=lax.Precision.HIGHEST)
        * math.sqrt(leaf_rows)
    ).astype(jnp.bfloat16)
    first = jnp.einsum("kst,ktu->kus", inverse_one, factor_leaf, precision=lax.Precision.HIGHEST)
    second = jnp.einsum("kst,ktu->kus", inverse_two, factor_one, precision=lax.Precision.HIGHEST)
    transfers = jnp.stack([first, second], axis=1)
    return (bases[0], bases[1], transfers)


def solution(mesh):
    return jax.shard_map(
        local,
        mesh=mesh,
        in_specs=(
            P(None, None, "col", "row"),
            P(None, "row"),
            P(None, ("row", "col")),
            P(None, ("row", "col")),
            P(("row", "col"), None, None, None),
            P(None, "col", None),
        ),
        out_specs=(
            P(None, ("row", "col")),
            P(None, ("row", "col")),
            P(None, None, ("row", "col"), None),
        ),
        check_vma=False,
    )
```

profile of v0, /device:TPU:98, one launch (start us, length us, event | category | flops | bytes accessed | tf_op | source)
XLA Modules:
  0.0 524.5 jit_solution(15192901601436697136)
XLA Ops:
  0.6 1.9 collective-permute-start.1
  2.6 2.4 collective-permute-start
  11.1 1.8 add_convert_fusion
  12.9 12.7 %copy.136 = bf16[2,16,128,128]{1,0,3,2:T(2,128)(2,1)} copy(bf16[2,16,128,128]{3,1,0,2:T(8,128)(2,1)S(1)} %add_convert_fusion) | data formatting | bytes 2097152 | tf_op jit(solution)/shard_map/reshape | solution.py:56
  25.6 11.2 %reshape.174 = bf16[16,2,16384]{2,1,0:T(2,128)(2,1)} reshape(bf16[16384,2,16]{2,1,0:T(2,128)(2,1)} %bitcast.127) | data formatting | bytes 2097152
  36.9 7.6 %all-to-all-start = ((bf16[16,2,16384]{2,1,0:T(2,128)(2,1)}), bf16[16,2,16384]{2,1,0:T(2,128)(2,1)}, u32[]{:S(2)}, u32[]{:S(2)}) async-start(bf16[16,2,16384]{2,1,0:T(2,128)(2,1)} %reshape.174), calls=%async_computation | async-start | bytes 2097152 | tf_op jit(solution)/shard_map/all_to_all | solution.py:58
  44.6 11.5 %convolution_bitcast_fusion = f32[8,18,256,128]{2,3,1,0:T(8,128)} fusion(bf16[8,18,128,128]{3,2,1,0:T(8,128)(2,1)} %param.12, bf16[256,8,128,1]{2,1,0,3:T(8,128)(2,1)S(1)} %bitcast.136), kind=kOutput, calls=%fused_computation.7 | convolution fusion | flops 1207959552 | bytes 24117248 | tf_op jit(solution)/shard_map/mda,duai->dumi/dot_general | solution.py:64
  56.1 22.1 %copy.108 = f32[8,18,256,128]{3,1,0,2:T(8,128)} copy(f32[8,18,256,128]{2,3,1,0:T(8,128)} %convolution_bitcast_fusion) | data formatting | bytes 37748736 | tf_op jit(solution)/shard_map/mda,duai->dumi/transpose | solution.py:64
  78.9 12.8 %convolution_bitcast_fusion.1 = f32[256,24,128]{2,1,0:T(8,128)S(1)} fusion(f32[8,18,256,128]{3,1,0,2:T(8,128)} %copy.108, s32[8,18]{1,0:T(8,128)S(1)} %bitcast_add_fusion.2), kind=kOutput, calls=%fused_computation.11 | convolution fusion | flops 1358957952 | bytes 22020672 | tf_op jit(solution)/shard_map/bkg,bksc->sgc/dot_general | solution.py:40
  91.7 2.4 copy.109
  94.1 2.4 copy.110
  97.7 4.1 collective-permute-start.3
  101.8 2.1 collective-permute-start.2
  106.2 6.4 %convert_bitcast_fusion = bf16[256,8,18,128]{3,2,1,0:T(8,128)(2,1)} fusion(bf16[256,24,128,1]{2,1,0,3:T(8,128)(2,1)S(1)} %bitcast.130, s32[8,18]{1,0:T(8,128)S(1)} %bitcast_add_fusion.2), kind=kOutput, calls=%fused_computation.4 | convolution fusion | flops 231214464 | bytes 11010624 | tf_op jit(solution)/shard_map/jhc,wct->wjht/dot_general | solution.py:78
  112.5 12.4 %fusion = f32[8,256,128,1]{1,2,3,0:T(8,128)} fusion(bf16[8,18,128,128]{3,2,1,0:T(8,128)(2,1)} %param.12, bf16[256,8,18,128]{3,2,1,0:T(8,128)(2,1)} %convert_bitcast_fusion), kind=kOutput, calls=%fused_computation.5 | convolution fusion | flops 1207959552 | bytes 15204352 | tf_op jit(solution)/shard_map/wjht,jhot->wjo/dot_general | solution.py:81
  125.0 2.6 copy.104
  127.6 8.9 %reshape.175 = bf16[16384,2,16]{2,1,0:T(2,128)(2,1)} reshape(bf16[16,2,16384]{2,1,0:T(2,128)(2,1)} %all-to-all-done) | data formatting | bytes 2097152
  136.5 12.7 %copy.137 = bf16[2,16,16,1024]{3,2,1,0:T(8,128)(2,1)} copy(bf16[2,16,16,1024]{1,0,3,2:T(2,128)(2,1)} %bitcast.128) | data formatting | bytes 2097152 | tf_op jit(solution)/shard_map/all_to_all | solution.py:58
  152.7 1.8 fusion.13
  154.5 2.3 fusion.57
  159.0 6.9 %collective-permute-done.4 = bf16[2,256,256]{1,2,0:T(8,128)(2,1)S(1)} collective-permute-done((bf16[2,256,256]{1,2,0:T(8,128)(2,1)S(1)}, bf16[2,256,256]{1,2,0:T(8,128)(2,1)S(1)}, u32[]{:S(2)}, u32[]{:S(2)}) %collective-permute-start.4) | collective-permute-done | bytes 262176 | tf_op jit(solution)/shard_map/ppermute | solution.py:35
  166.0 3.0 collective-permute-start.5
  170.4 5.6 %collective-permute-done.5 = bf16[2,256,256]{1,2,0:T(8,128)(2,1)S(1)} collective-permute-done((bf16[2,256,256]{1,2,0:T(8,128)(2,1)S(1)}, bf16[2,256,256]{1,2,0:T(8,128)(2,1)S(1)}, u32[]{:S(2)}, u32[]{:S(2)}) %collective-permute-start.5) | collective-permute-done | bytes 262176 | tf_op jit(solution)/shard_map/ppermute | solution.py:35
  180.4 70.6 %custom-call.17 = f32[6,128,128]{2,1,0:T(8,128)S(1)} custom-call(f32[6,128,128]{2,1,0:T(8,128)S(1)} %cholesky.122), custom_call_target="Cholesky" | custom-call | tf_op jit(solution)/shard_map/jit(cholesky)/cholesky | solution.py:99
  252.5 60.4 %custom-call.18 = f32[6,1,128,128]{2,3,1,0:T(8,128)} custom-call(f32[6,1,128,128]{3,2,1,0:T(8,128)} %select_bitcast_fusion), custom_call_target="InvertDiagBlocksLowerTriangular" | custom-call | tf_op jit(solution)/shard_map/jit(cholesky)/cholesky | solution.py:99
  316.1 71.1 %custom-call.19 = f32[6,128,128]{2,1,0:T(8,128)S(1)} custom-call(f32[6,128,128]{2,1,0:T(8,128)} %slice_subtract_fusion), custom_call_target="Cholesky" | custom-call | tf_op jit(solution)/shard_map/jit(cholesky)/cholesky | solution.py:99
  388.8 5.6 %while.1 = (s32[]{:T(128)}, f32[6,256,256]{2,1,0:T(8,128)S(1)}, s32[2,2]{1,0:T(2,128)S(1)}, f32[2,6,128,128]{3,2,0,1:T(8,128)}, s32[]{:T(128)}) while((s32[]{:T(128)}, f32[6,256,256]{2,1,0:T(8,128)S(1)}, s32[2,2]{1,0:T(2,128)S(1)}, f32[2,6,128,128]{3,2,0,1:T(8,128)}, s32[]{:T(128)}) %tuple.44), condition=%wide.while_cond, body=%wide.while_body.sunk | while | flops 2 | bytes 787565 | solution.py:101
  389.4 2.2 bitcast_dynamic-update-slice_fusion.2
  392.2 2.2 bitcast_dynamic-update-slice_fusion.2
  394.4 119.6 %custom-call.20 = f32[6,2,128,128]{2,3,1,0:T(8,128)} custom-call(f32[6,2,128,128]{3,2,1,0:T(8,128)} %bitcast.139), custom_call_target="InvertDiagBlocksLowerTriangular" | custom-call | tf_op jit(solution)/shard_map/vmap(jit(_solve_triangular))/triangular_solve | solution.py:101
  514.0 1.9 fusion.33
  517.6 2.0 multiply_convert_fusion
  (88 shorter events, 35.3 us)
Async XLA Ops:
  0.6 103.9 %collective-permute-start.1 = (bf16[256,1024]{1,0:T(8,128)(2,1)}, bf16[256,1024]{1,0:T(8,128)(2,1)}, u32[]{:S(2)}, u32[]{:S(2)}) collective-permute-start(bf16[256,1024]{1,0:T(8,128)(2,1)} %param.10), channel_id=1, source_target_pairs={{16,0},{32,16},{48,32},{64,48},{80,64},{96,80},{112,96},{128,112},... | collective-permute-start | bytes 1572872 | tf_op jit(solution)/shard_map/ppermute | solution.py:21
  2.6 102.0 %collective-permute-start = (bf16[256,1024]{1,0:T(8,128)(2,1)}, bf16[256,1024]{1,0:T(8,128)(2,1)}, u32[]{:S(2)}, u32[]{:S(2)}) collective-permute-start(bf16[256,1024]{1,0:T(8,128)(2,1)} %param.10), channel_id=1, source_target_pairs={{0,16},{16,32},{32,48},{48,64},{64,80},{80,96},{96,112},{112,128},... | collective-permute-start | bytes 1572872 | tf_op jit(solution)/shard_map/ppermute | solution.py:20
  6.9 0.7 copy-start.12
  36.9 7.6 %copy-start.8 = (bf16[256,1024]{1,0:T(8,128)(2,1)S(1)}, bf16[256,1024]{1,0:T(8,128)(2,1)}, u32[]{:S(2)}) copy-start(bf16[256,1024]{1,0:T(8,128)(2,1)} %param.11) | copy-start | bytes 1572868
  36.9 90.7 %all-to-all-start = ((bf16[16,2,16384]{2,1,0:T(2,128)(2,1)}), bf16[16,2,16384]{2,1,0:T(2,128)(2,1)}, u32[]{:S(2)}, u32[]{:S(2)}) async-start(bf16[16,2,16384]{2,1,0:T(2,128)(2,1)} %reshape.174), calls=%async_computation | async-start | bytes 2097152 | tf_op jit(solution)/shard_map/all_to_all | solution.py:58
  96.7 7.9 %copy-start.11 = (bf16[256,1024]{1,0:T(8,128)(2,1)S(1)}, bf16[256,1024]{1,0:T(8,128)(2,1)}, u32[]{:S(2)}) copy-start(bf16[256,1024]{1,0:T(8,128)(2,1)} %param.10) | copy-start | bytes 1572868
  97.7 54.9 %collective-permute-start.3 = (bf16[256,1024]{1,0:T(8,128)(2,1)}, bf16[256,1024]{1,0:T(8,128)(2,1)}, u32[]{:S(2)}, u32[]{:S(2)}) collective-permute-start(bf16[256,1024]{1,0:T(8,128)(2,1)} %get-tuple-element.48), channel_id=1, source_target_pairs={{0,16},{16,32},{32,48},{48,64},{64,80},{80,96},{96,112},{112,128},... | collective-permute-start | bytes 1572872 | tf_op jit(solution)/shard_map/ppermute | solution.py:29
  101.8 50.8 %collective-permute-start.2 = (bf16[256,1024]{1,0:T(8,128)(2,1)}, bf16[256,1024]{1,0:T(8,128)(2,1)}, u32[]{:S(2)}, u32[]{:S(2)}) collective-permute-start(bf16[256,1024]{1,0:T(8,128)(2,1)} %get-tuple-element.47), channel_id=1, source_target_pairs={{16,0},{32,16},{48,32},{64,48},{80,64},{96,80},{112,96},{128,112},... | collective-permute-start | bytes 1572872 | tf_op jit(solution)/shard_map/ppermute | solution.py:29
  151.3 1.2 copy-start.5
  152.6 1.8 copy-start
  154.5 4.5 copy-start.2
  156.8 9.2 %collective-permute-start.4 = (bf16[2,256,256]{1,2,0:T(8,128)(2,1)S(1)}, bf16[2,256,256]{1,2,0:T(8,128)(2,1)S(1)}, u32[]{:S(2)}, u32[]{:S(2)}) collective-permute-start(bf16[2,256,256]{1,2,0:T(8,128)(2,1)S(1)} %get-tuple-element.58), channel_id=1, source_target_pairs={{0,1},{1,0},{2,3},{3,2},{4,5},{5,4},{6,7},{7,6},{8,9},{9,8},{10,11... | collective-permute-start | bytes 786440 | tf_op jit(solution)/shard_map/ppermute | solution.py:35
  166.0 9.9 %collective-permute-start.5 = (bf16[2,256,256]{1,2,0:T(8,128)(2,1)S(1)}, bf16[2,256,256]{1,2,0:T(8,128)(2,1)S(1)}, u32[]{:S(2)}, u32[]{:S(2)}) collective-permute-start(bf16[2,256,256]{1,2,0:T(8,128)(2,1)S(1)} %get-tuple-element.37), channel_id=1, source_target_pairs={{0,2},{1,3},{2,0},{3,1},{4,6},{5,7},{6,4},{7,5},{8,10},{9,11},{10,... | collective-permute-start | bytes 786440 | tf_op jit(solution)/shard_map/ppermute | solution.py:35
  176.0 0.8 copy-start.4
  387.6 1.1 copy-start.13
  388.8 125.2 %copy-start.10 = (f32[128,256]{1,0:T(8,128)S(1)}, f32[128,256]{1,0:T(8,128)}, u32[]{:S(2)}) copy-start(f32[128,256]{1,0:T(8,128)} %get-tuple-element.55) | copy-start | bytes 393220
  388.8 127.1 %copy-start.9 = (f32[128,256]{1,0:T(8,128)S(1)}, f32[128,256]{1,0:T(8,128)}, u32[]{:S(2)}) copy-start(f32[128,256]{1,0:T(8,128)} %get-tuple-element.54) | copy-start | bytes 393220
  514.0 2.8 copy-start.7
  515.9 1.7 copy-start.1
  515.9 1.7 copy-start.3
  517.6 2.0 copy-start.6
where the time goes:
time: 535 us; the launch traced here: 524 us
  other arithmetic  336 us (63%)
  local copies, waits for them, and re-layouts  95.4 us (18%)
  matrix products  56.3 us (11%)
  starting transfers between devices  22.7 us (4%)
  waiting for transfers between devices  12.6 us (2%)
    another operation x10, other arithmetic, local(): factors = jnp.linalg.cholesky(stacked_grams)  205 us
    another operation x4, other arithmetic, local(): jax.vmap(partial(jax.scipy.linalg.solve_triangular, lower=True))  122 us
    unnamed x35, local copies, waits for them, and re-layouts  23.5 us
    transpose x1, local copies, waits for them, and re-layouts, local(): jnp.einsum('mda,duai->dumi', conjugate_transpose_rows, stored_sparse_bloc...  22.1 us
    dot_general x1, matrix products, spread_terms(): jnp.einsum('bkg,bksc->sgc', onehot, sketch_products, precision=lax.Precis...  12.8 us
    reshape x1, local copies, waits for them, and re-layouts, local(): (first_child + second_child).astype(jnp.bfloat16)  12.7 us
    all_to_all x1, local copies, waits for them, and re-layouts, local(): lax.all_to_all(extended, 'col', split_axis=2, concat_axis=1, tiled=True)  12.7 us
    ppermute x2, waiting for transfers between devices, from_partner(): return lax.ppermute(value, axis, pairs)  12.5 us
  transfers between devices with their start and end apart: 7, of which 2 were waited for; matrix products, arithmetic and copies ran while one was open for 26% of the time, Pallas kernels for 0%

commit v1 on v0

--- a/solution.py
+++ b/solution.py
@@ -55,7 +55,10 @@
     extended = (
         (first_child + second_child).astype(jnp.bfloat16).reshape(2, samples_here, rows_group)
     )
-    regrouped = lax.all_to_all(extended, "col", split_axis=2, concat_axis=1, tiled=True)
+    regrouped = jnp.concatenate(
+        lax.all_to_all(jnp.stack(jnp.split(extended, lax.axis_size("col"), axis=2)), "col", 0, 0),
+        axis=1,
+    )
     own_pattern = lax.dynamic_index_in_dim(block_pattern, row_pos, 0, keepdims=False)
     regions = jnp.arange(3 * SLOTS, dtype=jnp.int32) // SLOTS
     flat_index = regions[None, :] * leaf_blocks + own_pattern

time: 535 us -> 500 us (0.935)
  local copies, waits for them, and re-layouts: 95.4 us -> 64.5 us
    reshape x1 -> x0, local copies, waits for them, and re-layouts: 12.7 us -> none  [local(): (first_child + second_child).astype(jnp.bfloat16)]
    all_to_all x1 -> x0, local copies, waits for them, and re-layouts: 12.7 us -> none  [local(): lax.all_to_all(extended, 'col', split_axis=2, concat_axis=1, tiled=True)]
    unnamed x35 -> x46, local copies, waits for them, and re-layouts: 23.5 us -> 13.5 us
  transfers between devices with their start and end apart: 7 -> 7, of which waited for: 2 -> 2; matrix products, arithmetic and copies ran while one was open for 26% -> 21% of each run, Pallas kernels for 0% -> 0%
where the time goes in v1:
time: 500 us; the launch traced here: 491 us
  other arithmetic  334 us (67%)
  local copies, waits for them, and re-layouts  64.5 us (13%)
  matrix products  56.3 us (11%)
  starting transfers between devices  23.8 us (5%)
  waiting for transfers between devices  10.6 us (2%)
    another operation x10, other arithmetic, local(): factors = jnp.linalg.cholesky(stacked_grams)  204 us
    another operation x4, other arithmetic, local(): jax.vmap(partial(jax.scipy.linalg.solve_triangular, lower=True))  122 us
    transpose x1, local copies, waits for them, and re-layouts, local(): jnp.einsum('mda,duai->dumi', conjugate_transpose_rows, stored_sparse_bloc...  22.1 us
    unnamed x46, local copies, waits for them, and re-layouts  13.5 us
    dot_general x1, matrix products, spread_terms(): jnp.einsum('bkg,bksc->sgc', onehot, sketch_products, precision=lax.Precis...  12.8 us
    dot_general x1, matrix products, local(): jnp.einsum('wjht,jhot->wjo', collected_samples, stored_sparse_blocks, pre...  12.4 us
    dot_general x1, matrix products, local(): jnp.einsum('mda,duai->dumi', conjugate_transpose_rows, stored_sparse_bloc...  11.5 us
    ppermute x2, waiting for transfers between devices, from_partner(): return lax.ppermute(value, axis, pairs)  10.6 us
  transfers between devices with their start and end apart: 7, of which 2 were waited for; matrix products, arithmetic and copies ran while one was open for 21% of the time, Pallas kernels for 0%

profile of v1, /device:TPU:98, one launch (start us, length us, event | category | flops | bytes accessed | tf_op | source)
XLA Modules:
  0.0 490.9 jit_solution(12330021450137008400)
XLA Ops:
  0.6 1.9 collective-permute-start.1
  2.6 2.4 collective-permute-start
  6.1 11.5 %convolution_bitcast_fusion = f32[8,18,256,128]{2,3,1,0:T(8,128)} fusion(bf16[8,18,128,128]{3,2,1,0:T(8,128)(2,1)} %param.12, bf16[256,8,128,1]{2,1,0,3:T(8,128)(2,1)S(1)} %bitcast.201), kind=kOutput, calls=%fused_computation.7 | convolution fusion | flops 1207959552 | bytes 24117248 | tf_op jit(solution)/shard_map/mda,duai->dumi/dot_general | solution.py:67
  17.6 22.1 %copy.102 = f32[8,18,256,128]{3,1,0,2:T(8,128)} copy(f32[8,18,256,128]{2,3,1,0:T(8,128)} %convolution_bitcast_fusion) | data formatting | bytes 37748736 | tf_op jit(solution)/shard_map/mda,duai->dumi/transpose | solution.py:67
  40.4 12.8 %convolution_bitcast_fusion.1 = f32[256,24,128]{2,1,0:T(8,128)S(1)} fusion(f32[8,18,256,128]{3,1,0,2:T(8,128)} %copy.102, s32[8,18]{1,0:T(8,128)S(1)} %bitcast_add_fusion.1), kind=kOutput, calls=%fused_computation.11 | convolution fusion | flops 1358957952 | bytes 22020672 | tf_op jit(solution)/shard_map/bkg,bksc->sgc/dot_general | solution.py:40
  53.2 2.4 copy.103
  55.6 2.4 copy.104
  59.3 4.6 collective-permute-start.3
  63.9 1.9 collective-permute-start.2
  69.8 3.0 gather_fusion.1
  72.8 3.0 gather_fusion
  75.8 1.9 copy_bitcast_fusion
  87.8 8.1 %all-to-all-start = ((bf16[16,2,16,1024]{3,2,1,0:T(8,128)(2,1)}), bf16[16,2,16,1024]{3,2,1,0:T(8,128)(2,1)}, u32[]{:S(2)}, u32[]{:S(2)}) async-start(bf16[16,2,16,1024]{3,2,1,0:T(8,128)(2,1)} %fusion.43), calls=%async_computation | async-start | bytes 2097152 | tf_op jit(solution)/shard_map/all_to_all | solution.py:59
  98.3 6.4 %convert_bitcast_fusion = bf16[256,8,18,128]{3,2,1,0:T(8,128)(2,1)} fusion(bf16[256,24,128,1]{2,1,0,3:T(8,128)(2,1)S(1)} %bitcast.196, s32[8,18]{1,0:T(8,128)S(1)} %bitcast_add_fusion.1), kind=kOutput, calls=%fused_computation.4 | convolution fusion | flops 231214464 | bytes 11010624 | tf_op jit(solution)/shard_map/jhc,wct->wjht/dot_general | solution.py:81
  104.7 12.4 %fusion = f32[8,256,128,1]{1,2,3,0:T(8,128)} fusion(bf16[8,18,128,128]{3,2,1,0:T(8,128)(2,1)} %param.12, bf16[256,8,18,128]{3,2,1,0:T(8,128)(2,1)} %convert_bitcast_fusion), kind=kOutput, calls=%fused_computation.5 | convolution fusion | flops 1207959552 | bytes 15204352 | tf_op jit(solution)/shard_map/wjht,jhot->wjo/dot_general | solution.py:84
  117.0 2.6 copy.99
  121.3 1.9 fusion.14
  123.2 2.3 fusion.75
  127.8 6.0 %collective-permute-done.4 = bf16[2,256,256]{1,2,0:T(8,128)(2,1)S(1)} collective-permute-done((bf16[2,256,256]{1,2,0:T(8,128)(2,1)S(1)}, bf16[2,256,256]{1,2,0:T(8,128)(2,1)S(1)}, u32[]{:S(2)}, u32[]{:S(2)}) %collective-permute-start.4) | collective-permute-done | bytes 262176 | tf_op jit(solution)/shard_map/ppermute | solution.py:35
  133.8 3.2 collective-permute-start.5
  138.3 4.6 collective-permute-done.5
  145.5 1.7 fusion.7
  147.3 70.3 %custom-call.17 = f32[6,128,128]{2,1,0:T(8,128)S(1)} custom-call(f32[6,128,128]{2,1,0:T(8,128)S(1)} %cholesky.122), custom_call_target="Cholesky" | custom-call | tf_op jit(solution)/shard_map/jit(cholesky)/cholesky | solution.py:102
  219.2 60.4 %custom-call.18 = f32[6,1,128,128]{2,3,1,0:T(8,128)} custom-call(f32[6,1,128,128]{3,2,1,0:T(8,128)} %select_bitcast_fusion), custom_call_target="InvertDiagBlocksLowerTriangular" | custom-call | tf_op jit(solution)/shard_map/jit(cholesky)/cholesky | solution.py:102
  281.1 1.7 slice_subtract_fusion
  282.8 71.1 %custom-call.19 = f32[6,128,128]{2,1,0:T(8,128)S(1)} custom-call(f32[6,128,128]{2,1,0:T(8,128)} %slice_subtract_fusion), custom_call_target="Cholesky" | custom-call | tf_op jit(solution)/shard_map/jit(cholesky)/cholesky | solution.py:102
  355.5 5.6 %while.1 = (s32[]{:T(128)}, f32[6,256,256]{2,1,0:T(8,128)S(1)}, s32[2,2]{1,0:T(2,128)S(1)}, f32[2,6,128,128]{3,2,0,1:T(8,128)}, s32[]{:T(128)}) while((s32[]{:T(128)}, f32[6,256,256]{2,1,0:T(8,128)S(1)}, s32[2,2]{1,0:T(2,128)S(1)}, f32[2,6,128,128]{3,2,0,1:T(8,128)}, s32[]{:T(128)}) %tuple.43), condition=%wide.while_cond, body=%wide.while_body.sunk | while | flops 2 | bytes 787565 | solution.py:104
  356.1 2.2 bitcast_dynamic-update-slice_fusion.2
  358.9 2.2 bitcast_dynamic-update-slice_fusion.2
  361.1 119.5 %custom-call.20 = f32[6,2,128,128]{2,3,1,0:T(8,128)} custom-call(f32[6,2,128,128]{3,2,1,0:T(8,128)} %bitcast.205), custom_call_target="InvertDiagBlocksLowerTriangular" | custom-call | tf_op jit(solution)/shard_map/vmap(jit(_solve_triangular))/triangular_solve | solution.py:104
  480.7 1.9 fusion.34
  484.3 2.0 multiply_convert_fusion
  (96 shorter events, 39.3 us)
Async XLA Ops:
  0.6 95.9 %collective-permute-start.1 = (bf16[256,1024]{1,0:T(8,128)(2,1)}, bf16[256,1024]{1,0:T(8,128)(2,1)}, u32[]{:S(2)}, u32[]{:S(2)}) collective-permute-start(bf16[256,1024]{1,0:T(8,128)(2,1)} %param.10), channel_id=1, source_target_pairs={{16,0},{32,16},{48,32},{64,48},{80,64},{96,80},{112,96},{128,112},... | collective-permute-start | bytes 1572872 | tf_op jit(solution)/shard_map/ppermute | solution.py:21
  2.6 93.9 %collective-permute-start = (bf16[256,1024]{1,0:T(8,128)(2,1)}, bf16[256,1024]{1,0:T(8,128)(2,1)}, u32[]{:S(2)}, u32[]{:S(2)}) collective-permute-start(bf16[256,1024]{1,0:T(8,128)(2,1)} %param.10), channel_id=1, source_target_pairs={{0,16},{16,32},{32,48},{48,64},{64,80},{80,96},{96,112},{112,128},... | collective-permute-start | bytes 1572872 | tf_op jit(solution)/shard_map/ppermute | solution.py:20
  58.2 7.6 %copy-start.6 = (bf16[2,2,16,16384]{3,2,1,0:T(8,128)(2,1)S(1)}, bf16[2,2,16,16384]{3,2,1,0:T(8,128)(2,1)}, u32[]{:S(2)}) copy-start(bf16[2,2,16,16384]{3,2,1,0:T(8,128)(2,1)} %param.8) | copy-start | bytes 6291460
  59.3 62.0 %collective-permute-start.3 = (bf16[256,1024]{1,0:T(8,128)(2,1)}, bf16[256,1024]{1,0:T(8,128)(2,1)}, u32[]{:S(2)}, u32[]{:S(2)}) collective-permute-start(bf16[256,1024]{1,0:T(8,128)(2,1)} %get-tuple-element.45), channel_id=1, source_target_pairs={{0,16},{16,32},{32,48},{48,64},{64,80},{80,96},{96,112},{112,128},... | collective-permute-start | bytes 1572872 | tf_op jit(solution)/shard_map/ppermute | solution.py:29
  63.9 57.4 %collective-permute-start.2 = (bf16[256,1024]{1,0:T(8,128)(2,1)}, bf16[256,1024]{1,0:T(8,128)(2,1)}, u32[]{:S(2)}, u32[]{:S(2)}) collective-permute-start(bf16[256,1024]{1,0:T(8,128)(2,1)} %get-tuple-element.44), channel_id=1, source_target_pairs={{16,0},{32,16},{48,32},{64,48},{80,64},{96,80},{112,96},{128,112},... | collective-permute-start | bytes 1572872 | tf_op jit(solution)/shard_map/ppermute | solution.py:29
  66.2 1.7 copy-start.11
  87.8 31.8 %all-to-all-start = ((bf16[16,2,16,1024]{3,2,1,0:T(8,128)(2,1)}), bf16[16,2,16,1024]{3,2,1,0:T(8,128)(2,1)}, u32[]{:S(2)}, u32[]{:S(2)}) async-start(bf16[16,2,16,1024]{3,2,1,0:T(8,128)(2,1)} %fusion.43), calls=%async_computation | async-start | bytes 2097152 | tf_op jit(solution)/shard_map/all_to_all | solution.py:59
  119.6 1.5 copy-start.5
  121.3 1.9 copy-start.2
  123.2 4.6 copy-start
  125.5 8.2 %collective-permute-start.4 = (bf16[2,256,256]{1,2,0:T(8,128)(2,1)S(1)}, bf16[2,256,256]{1,2,0:T(8,128)(2,1)S(1)}, u32[]{:S(2)}, u32[]{:S(2)}) collective-permute-start(bf16[2,256,256]{1,2,0:T(8,128)(2,1)S(1)} %get-tuple-element.55), channel_id=1, source_target_pairs={{0,1},{1,0},{2,3},{3,2},{4,5},{5,4},{6,7},{7,6},{8,9},{9,8},{10,11... | collective-permute-start | bytes 786440 | tf_op jit(solution)/shard_map/ppermute | solution.py:35
  133.8 9.1 %collective-permute-start.5 = (bf16[2,256,256]{1,2,0:T(8,128)(2,1)S(1)}, bf16[2,256,256]{1,2,0:T(8,128)(2,1)S(1)}, u32[]{:S(2)}, u32[]{:S(2)}) collective-permute-start(bf16[2,256,256]{1,2,0:T(8,128)(2,1)S(1)} %get-tuple-element.34), channel_id=1, source_target_pairs={{0,2},{1,3},{2,0},{3,1},{4,6},{5,7},{6,4},{7,5},{8,10},{9,11},{10,... | collective-permute-start | bytes 786440 | tf_op jit(solution)/shard_map/ppermute | solution.py:35
  142.9 0.8 copy-start.4
  354.3 1.1 copy-start.12
  355.5 125.2 %copy-start.10 = (f32[128,256]{1,0:T(8,128)S(1)}, f32[128,256]{1,0:T(8,128)}, u32[]{:S(2)}) copy-start(f32[128,256]{1,0:T(8,128)} %get-tuple-element.52) | copy-start | bytes 393220
  355.5 127.1 %copy-start.9 = (f32[128,256]{1,0:T(8,128)S(1)}, f32[128,256]{1,0:T(8,128)}, u32[]{:S(2)}) copy-start(f32[128,256]{1,0:T(8,128)} %get-tuple-element.51) | copy-start | bytes 393220
  480.7 2.8 copy-start.8
  482.6 1.7 copy-start.1
  482.6 1.7 copy-start.3
  484.3 2.0 copy-start.7
